TPU v7x, 512 devices: a whole 4x4x16 slice. The times are simulated.
512 devices in a mesh: dp: 8 (over z_hi, x), space: 64 (over y, z_lo, core).
Axes of the slice: x: 4, y: 4, z: 16 (z_hi: 2, z_lo: 8; z = z_hi * 8 + z_lo), core: 2. Of those that a mesh axis runs over, the one named last changes fastest.
Arguments:
- queries: bfloat16 [8, 24576, 768], P('dp', 'space'), may hold values from -6 to 6, as said below
- keys: bfloat16 [8, 24576, 768], P('dp', 'space'), may hold values from -6 to 6, as said below
- values: bfloat16 [8, 24576, 768], P('dp', 'space'), may hold values from -6 to 6
- out_grad: bfloat16 [8, 24576, 768], P('dp', 'space'), may hold values from -6 to 6
- w_out: bfloat16 [768, 768], P('dp'), may hold values from -0.21875 to 0.21875
- neighbours: int32 [192, 9], P('space'), may hold values from 0 to 191, as said below
- live_count: int32 [192], P('space'), may hold values from 7 to 9
Outputs:
- query_grad: bfloat16 [8, 24576, 768], P('dp', 'space')
- key_grad: bfloat16 [8, 24576, 768], P('dp', 'space')
- value_grad: bfloat16 [8, 24576, 768], P('dp', 'space')
- weight_grad: float32 [768, 768], P('dp')
Inputs may be any that keep to these rules, and one draw needn't show every extreme that they name: `queries`: mostly of order one. `keys`: mostly of order one. `neighbours`: slot 0 of block b is b itself; the slots of a row name distinct blocks, all held by the same tile as b or by the tiles one index lower or higher along space, cyclically. Slots from live_count on hold valid ids that are ignored.
All inputs are finite; a program needn't handle non-finite values.
Results may differ from a plain program's by a relative error of at most 0.022.
Values may be sent and summed in bfloat16 or wider, within the bound.
No kernel may reach another device: no remote copies, remote signals or barrier semaphores. Data moves between devices by JAX's collectives and lax.ppermute only.
A program may use at most 64 MiB of HBM per device.

v0:
```python
import math

import jax
import jax.numpy as jnp
from jax import lax
from jax.sharding import PartitionSpec as P

HEADS = 12
HD = 64
BLK = 128
NB = 9
HGROUP = 4


def shifted(block, axis, distance):
    devices = range(lax.axis_size(axis))
    route = [((i - distance) % len(devices), i) for i in devices]
    return lax.ppermute(block, axis, route)


def body(queries, keys, values, out_grad, w_out, neighbours, live_count):
    query_rows = queries[0]
    key_rows = keys[0]
    value_rows = values[0]
    grad_rows = out_grad[0]
    tokens, width = query_rows.shape
    nblock = tokens // BLK
    groups = HEADS // HGROUP
    group_width = HGROUP * HD
    n_space = lax.axis_size("space")
    index = lax.axis_index("space")
    total = nblock * n_space
    scale = 1.0 / math.sqrt(HD)
    paired = jnp.stack([key_rows, value_rows])
    before = shifted(paired, "space", 1)
    after = shifted(paired, "space", -1)
    window = jnp.concatenate([before, paired, after], axis=1)
    window = window.reshape(2, 3 * nblock, BLK, width)
    full_w = lax.all_gather(w_out, "dp", axis=0, tiled=True)
    d_attended = lax.dot_general(
        grad_rows, full_w, (((1,), (1,)), ((), ())), preferred_element_type=jnp.float32
    ).astype(jnp.bfloat16)
    local_ids = jnp.mod(neighbours - (index - 1) * nblock, total)
    slot_live = jnp.arange(NB)[None, :] < live_count[:, None]

    def step_fn(carry, step):
        block = step // groups
        group = step % groups
        column = group * group_width
        query_blk = lax.dynamic_slice(query_rows, (block * BLK, column), (BLK, group_width))
        dout_blk = lax.dynamic_slice(d_attended, (block * BLK, column), (BLK, group_width))
        ids = lax.dynamic_index_in_dim(local_ids, block, 0, keepdims=False)
        live = lax.dynamic_index_in_dim(slot_live, block, 0, keepdims=False)
        group_win = lax.dynamic_slice_in_dim(window, column, group_width, 3)
        picked = group_win[:, ids]
        key_blk = picked[0].reshape(NB * BLK, HGROUP, HD)
        val_blk = picked[1].reshape(NB * BLK, HGROUP, HD)
        query_heads = query_blk.reshape(BLK, HGROUP, HD)
        dout_heads = dout_blk.reshape(BLK, HGROUP, HD)
        scores = (
            jnp.einsum("qhd,khd->hqk", query_heads, key_blk, preferred_element_type=jnp.float32)
            * scale
        )
        keymask = jnp.repeat(live, BLK)
        scores = jnp.where(keymask[None, None, :], scores, -1e30)
        top = jnp.max(scores, axis=-1, keepdims=True)
        expo = jnp.exp(scores - top)
        probs = expo / jnp.sum(expo, axis=-1, keepdims=True)
        probs_half = probs.astype(jnp.bfloat16)
        attended = jnp.einsum(
            "hqk,khd->qhd", probs_half, val_blk, preferred_element_type=jnp.float32
        ).astype(jnp.bfloat16)
        delta = jnp.sum(dout_heads.astype(jnp.float32) * attended.astype(jnp.float32), axis=-1)
        dprobs = jnp.einsum("qhd,khd->hqk", dout_heads, val_blk, preferred_element_type=jnp.float32)
        dscores = (probs * (dprobs - delta.T[:, :, None])).astype(jnp.bfloat16)
        dquery = (
            jnp.einsum("hqk,khd->qhd", dscores, key_blk, preferred_element_type=jnp.float32) * scale
        ).astype(jnp.bfloat16)
        dkey = (
            jnp.einsum("hqk,qhd->khd", dscores, query_heads, preferred_element_type=jnp.float32)
            * scale
        )
        dval = jnp.einsum(
            "hqk,qhd->khd", probs_half, dout_heads, preferred_element_type=jnp.float32
        )
        terms = jnp.stack(
            [dkey.reshape(NB, BLK, group_width), dval.reshape(NB, BLK, group_width)], axis=1
        )
        carry = carry.at[group, ids].add(terms)
        return (carry, (attended.reshape(BLK, group_width), dquery.reshape(BLK, group_width)))

    start_sums = jnp.zeros((groups, 3 * nblock, 2, BLK, group_width), jnp.float32)
    sums, (attended_all, dquery_all) = lax.scan(step_fn, start_sums, jnp.arange(nblock * groups))
    attended_rows = (
        attended_all.reshape(nblock, groups, BLK, group_width)
        .transpose(0, 2, 1, 3)
        .reshape(tokens, width)
    )
    dquery_rows = (
        dquery_all.reshape(nblock, groups, BLK, group_width)
        .transpose(0, 2, 1, 3)
        .reshape(tokens, width)
    )
    sums = sums.transpose(2, 1, 3, 0, 4).reshape(2, 3 * tokens, width)
    lower_half = sums[:, :tokens].astype(jnp.bfloat16)
    own_terms = sums[:, tokens : 2 * tokens]
    upper_half = sums[:, 2 * tokens :].astype(jnp.bfloat16)
    from_before = shifted(upper_half, "space", 1)
    from_after = shifted(lower_half, "space", -1)
    grads = (own_terms + from_before.astype(jnp.float32) + from_after.astype(jnp.float32)).astype(
        jnp.bfloat16
    )
    weight_term = lax.dot_general(
        attended_rows, grad_rows, (((0,), (0,)), ((), ())), preferred_element_type=jnp.float32
    )
    reduced = lax.psum_scatter(
        weight_term.astype(jnp.bfloat16), "dp", scatter_dimension=0, tiled=True
    ).astype(jnp.float32)
    weight_grad = lax.psum(reduced, "space")
    return (dquery_rows[None], grads[0][None], grads[1][None], weight_grad)


def solution(mesh):
    return jax.shard_map(
        body,
        mesh=mesh,
        in_specs=(
            P("dp", "space", None),
            P("dp", "space", None),
            P("dp", "space", None),
            P("dp", "space", None),
            P("dp", None),
            P("space", None),
            P("space"),
        ),
        out_specs=(
            P("dp", "space", None),
            P("dp", "space", None),
            P("dp", "space", None),
            P("dp", None),
        ),
        check_vma=False,
    )
```

profile of v0, /device:TPU:6, one launch (start us, length us, event | category | flops | bytes accessed | tf_op | source)
XLA Modules:
  0.0 1072.4 jit_solution(14839920909900036542)
XLA Ops:
  10.2 15.0 %collective-permute-start.1 = (bf16[2,384,768]{2,1,0:T(8,128)(2,1)S(1)}, bf16[2,384,768]{2,1,0:T(8,128)(2,1)S(1)}, u32[]{:S(2)}, u32[]{:S(2)}) collective-permute-start(bf16[2,384,768]{2,1,0:T(8,128)(2,1)S(1)} %constant_dynamic-update-slice_fusion.2), channel_id=1, source_target_pairs={{1,0},{2,1},{3,2},{4,3},{5,4},{6,5},{7,6},{8,7},{9,8},{10,9},{11,1... | collective-permute-start | bytes 3538952 | tf_op jit(solution)/shard_map/ppermute | solution.py:18
  28.4 18.0 %collective-permute-done.1 = bf16[2,384,768]{2,1,0:T(8,128)(2,1)S(1)} collective-permute-done((bf16[2,384,768]{2,1,0:T(8,128)(2,1)S(1)}, bf16[2,384,768]{2,1,0:T(8,128)(2,1)S(1)}, u32[]{:S(2)}, u32[]{:S(2)}) %collective-permute-start.1) | collective-permute-done | bytes 1179680 | tf_op jit(solution)/shard_map/ppermute | solution.py:18
  46.4 10.2 collective-permute-done
  59.7 61.4 %all-gather.2.cloned.1.call-done = bf16[768,768]{1,0:T(8,128)(2,1)} async-done(((bf16[96,768]{1,0:T(8,128)(2,1)}), bf16[768,768]{1,0:T(8,128)(2,1)}) %all-gather.2.cloned.1.call-update) | async-done | bytes 1179664 | tf_op jit(solution)/shard_map/all_gather | solution.py:39
  124.3 3.8 broadcast_in_dim.53
  128.1 387.0 %while.16 = (s32[]{:T(128)}, f32[3,9,2,128,256]{4,3,2,1,0:T(8,128)}, bf16[9,128,256]{1,2,0:T(8,128)(2,1)}, bf16[9,128,256]{1,2,0:T(8,128)(2,1)}, s32[9]{0:T(128)...) while((s32[]{:T(128)}, ...), condition=%wide.region_5.6_spmd, body=%wide.region_0.5_spmd.sunk | while | flops 460588800 | bytes 62997648 | solution.py:93
  155.2 3.8 pad_maximum_fusion.3
  163.1 7.9 scatter_fusion
  198.1 3.8 pad_maximum_fusion.3
  205.9 8.1 scatter_fusion
  241.1 3.8 pad_maximum_fusion.3
  249.0 8.1 scatter_fusion
  284.2 3.8 pad_maximum_fusion.3
  288.1 3.3 copy.45
  292.1 7.9 scatter_fusion
  327.0 3.8 pad_maximum_fusion.3
  334.9 8.1 scatter_fusion
  370.1 3.8 pad_maximum_fusion.3
  378.0 8.2 scatter_fusion
  413.2 3.8 pad_maximum_fusion.3
  421.1 7.9 scatter_fusion
  456.1 3.8 pad_maximum_fusion.3
  463.9 8.1 scatter_fusion
  499.1 3.8 pad_maximum_fusion.3
  507.0 8.1 scatter_fusion
  518.9 11.5 %copy.32 = f32[2,9,128,3,256]{4,3,2,1,0:T(4,128)} copy(f32[2,9,128,3,256]{4,2,0,1,3:T(8,128)} %bitcast.135) | data formatting | bytes 14155776 | tf_op jit(solution)/shard_map/transpose | solution.py:104
  530.4 12.0 %reshape.101 = f32[2,1152,768]{2,1,0:T(8,128)} reshape(f32[2,9,128,3,256]{4,3,2,1,0:T(4,128)} %copy.32) | data formatting | bytes 14155776 | tf_op jit(solution)/shard_map/reshape | solution.py:104
  542.4 3.4 convert.4
  549.3 12.4 %collective-permute-start.3 = (bf16[2,384,768]{2,1,0:T(8,128)(2,1)}, bf16[2,384,768]{2,1,0:T(8,128)(2,1)}, u32[]{:S(2)}, u32[]{:S(2)}) collective-permute-start(bf16[2,384,768]{2,1,0:T(8,128)(2,1)} %get-tuple-element.198), channel_id=1, source_target_pairs={{1,0},{2,1},{3,2},{4,3},{5,4},{6,5},{7,6},{8,7},{9,8},{10,9},{11,1... | collective-permute-start | bytes 3538952 | tf_op jit(solution)/shard_map/ppermute | solution.py:18
  563.7 32.1 %collective-permute-done.2 = bf16[2,384,768]{2,1,0:T(8,128)(2,1)S(1)} collective-permute-done((bf16[2,384,768]{2,1,0:T(8,128)(2,1)}, bf16[2,384,768]{2,1,0:T(8,128)(2,1)S(1)}, u32[]{:S(2)}, u32[]{:S(2)}) %collective-permute-start.2) | collective-permute-done | bytes 1179680 | tf_op jit(solution)/shard_map/ppermute | solution.py:18
  599.3 43.2 %reduce-scatter.2.cloned.1.call-done = bf16[96,768]{1,0:T(8,128)(2,1)} async-done(((bf16[768,768]{1,0:T(8,128)(2,1)}), bf16[96,768]{1,0:T(8,128)(2,1)}) %reduce-scatter.2.cloned.1.call-update) | async-done | bytes 147472 | tf_op jit(solution)/shard_map/reduce_scatter | solution.py:116
  642.5 423.0 %all-reduce.2 = f32[96,768]{1,0:T(8,128)} all-reduce(bf16[96,768]{1,0:T(8,128)(2,1)} %reduce-scatter.2.cloned.1.call-done), channel_id=1, replica_groups=mesh['dp'=8,'space'=64] {'space'}, use_global_device_ids=true, to_apply=%region_7.8 | all-reduce | flops 73728 | bytes 442368 | tf_op jit(solution)/shard_map/psum | solution.py:119
  (322 shorter events, 282.6 us)
Async XLA Ops:
  7.2 113.9 %copy-start = (bf16[1,384,768]{2,1,0:T(8,128)(2,1)S(1)}, bf16[1,384,768]{2,1,0:T(8,128)(2,1)}, u32[]{:S(2)}) copy-start(bf16[1,384,768]{2,1,0:T(8,128)(2,1)} %param.12) | copy-start | bytes 1769476
  7.2 20.0 %copy-start.4 = (bf16[1,384,768]{2,1,0:T(8,128)(2,1)S(1)}, bf16[1,384,768]{2,1,0:T(8,128)(2,1)}, u32[]{:S(2)}) copy-start(bf16[1,384,768]{2,1,0:T(8,128)(2,1)} %param.9) | copy-start | bytes 1769476
  7.2 21.1 %copy-start.7 = (s32[3]{0:T(128)S(1)}, s32[3]{0:T(128)}, u32[]{:S(2)}) copy-start(s32[3]{0:T(128)} %param.15) | copy-start | bytes 40
  7.2 21.2 %copy-start.6 = (s32[3,9]{1,0:T(4,128)S(1)}, s32[3,9]{1,0:T(4,128)}, u32[]{:S(2)}) copy-start(s32[3,9]{1,0:T(4,128)} %param.14) | copy-start | bytes 328
  7.2 113.8 %all-gather.2.cloned.1.call-start = ((), (), s32[]{:S(2)}) async-start(), calls=%async_computation.1 | async-start | bytes 1327104 | tf_op jit(solution)/shard_map/all_gather | solution.py:39
  7.9 634.6 %reduce-scatter.2.cloned.1.call-start = ((), (), s32[]{:S(2)}) async-start(), calls=%async_computation.2 | async-start | bytes 1327104 | tf_op jit(solution)/shard_map/reduce_scatter | solution.py:116
  10.2 36.2 %collective-permute-start.1 = (bf16[2,384,768]{2,1,0:T(8,128)(2,1)S(1)}, bf16[2,384,768]{2,1,0:T(8,128)(2,1)S(1)}, u32[]{:S(2)}, u32[]{:S(2)}) collective-permute-start(bf16[2,384,768]{2,1,0:T(8,128)(2,1)S(1)} %constant_dynamic-update-slice_fusion.2), channel_id=1, source_target_pairs={{1,0},{2,1},{3,2},{4,3},{5,4},{6,5},{7,6},{8,7},{9,8},{10,9},{11,1... | collective-permute-start | bytes 3538952 | tf_op jit(solution)/shard_map/ppermute | solution.py:18
  25.3 31.4 %collective-permute-start = (bf16[2,384,768]{2,1,0:T(8,128)(2,1)S(1)}, bf16[2,384,768]{2,1,0:T(8,128)(2,1)}, u32[]{:S(2)}, u32[]{:S(2)}) collective-permute-start(bf16[2,384,768]{2,1,0:T(8,128)(2,1)S(1)} %constant_dynamic-update-slice_fusion.2), channel_id=1, source_target_pairs={{63,0},{0,1},{1,2},{2,3},{3,4},{4,5},{5,6},{6,7},{7,8},{8,9},{9,10... | collective-permute-start | bytes 3538952 | tf_op jit(solution)/shard_map/ppermute | solution.py:18
  144.7 2.0 copy-start.2
  146.7 1.9 copy-start.1
  148.6 1.1 copy-start.3
  187.6 2.0 copy-start.2
  189.5 1.9 copy-start.1
  191.5 1.1 copy-start.3
  230.6 2.0 copy-start.2
  232.6 1.9 copy-start.1
  273.7 2.0 copy-start.2
  275.7 1.9 copy-start.1
  316.5 2.0 copy-start.2
  318.5 1.9 copy-start.1
  359.6 2.0 copy-start.2
  361.6 1.9 copy-start.1
  363.5 1.1 copy-start.3
  402.7 2.0 copy-start.2
  404.7 1.9 copy-start.1
  445.6 2.0 copy-start.2
  447.5 1.9 copy-start.1
  488.6 2.0 copy-start.2
  490.6 1.9 copy-start.1
  545.8 15.9 %copy-start.5 = (bf16[9,128,256]{1,2,0:T(8,128)(2,1)S(1)}, bf16[9,128,256]{1,2,0:T(8,128)(2,1)}, u32[]{:S(2)}) copy-start(bf16[9,128,256]{1,2,0:T(8,128)(2,1)} %get-tuple-element.134) | copy-start | bytes 1769476
  547.4 48.5 %collective-permute-start.2 = (bf16[2,384,768]{2,1,0:T(8,128)(2,1)}, bf16[2,384,768]{2,1,0:T(8,128)(2,1)S(1)}, u32[]{:S(2)}, u32[]{:S(2)}) collective-permute-start(bf16[2,384,768]{2,1,0:T(8,128)(2,1)} %get-tuple-element.197), channel_id=1, source_target_pairs={{63,0},{0,1},{1,2},{2,3},{3,4},{4,5},{5,6},{6,7},{7,8},{8,9},{9,10... | collective-permute-start | bytes 3538952 | tf_op jit(solution)/shard_map/ppermute | solution.py:18
  549.3 46.6 %collective-permute-start.3 = (bf16[2,384,768]{2,1,0:T(8,128)(2,1)}, bf16[2,384,768]{2,1,0:T(8,128)(2,1)}, u32[]{:S(2)}, u32[]{:S(2)}) collective-permute-start(bf16[2,384,768]{2,1,0:T(8,128)(2,1)} %get-tuple-element.198), channel_id=1, source_target_pairs={{1,0},{2,1},{3,2},{4,3},{5,4},{6,5},{7,6},{8,7},{9,8},{10,9},{11,1... | collective-permute-start | bytes 3538952 | tf_op jit(solution)/shard_map/ppermute | solution.py:18
  (6 other events, 6.8 us)
Sparse Core Ops, SparseCore 0:
  11.2 109.7 all-gather.1
  519.0 123.4 reduce-scatter.1
where the time goes:
time: 1080 us; the launch traced here: 1070 us
  blocking collectives  423 us (39%)
  local copies, waits for them, and re-layouts  213 us (20%)
  waiting for transfers between devices  166 us (15%)
  other arithmetic  134 us (12%)
  matrix products  72.8 us (7%)
  starting transfers between devices  31.3 us (3%)
  loops' own time  19 us (2%)
  between operations  14.2 us (1%)
    psum x1, blocking collectives, body(): weight_grad = lax.psum(reduced, 'space')  423 us
    scatter-add x9, other arithmetic, step_fn(): carry = carry.at[group, ids].add(terms)  72.5 us
    all_gather x1, waiting for transfers between devices, body(): full_w = lax.all_gather(w_out, 'dp', axis=0, tiled=True)  61.4 us
    ppermute x4, waiting for transfers between devices, shifted(): return lax.ppermute(block, axis, route)  60.4 us
    reduce_scatter x1, waiting for transfers between devices, body(): lax.psum_scatter(weight_term.astype(jnp.bfloat16), 'dp', scatter_dimensio...  43.2 us
    reshape x18, local copies, waits for them, and re-layouts, step_fn(): jnp.stack([dkey.reshape(NB, BLK, group_width), dval.reshape(NB, BLK, grou...  36.1 us
    another operation x9, other arithmetic, step_fn(): jnp.stack([dkey.reshape(NB, BLK, group_width), dval.reshape(NB, BLK, grou...  34.6 us
    ppermute x4, starting transfers between devices, shifted(): return lax.ppermute(block, axis, route)  31.2 us
  transfers between devices with their start and end apart: 6, of which 5 were waited for; matrix products, arithmetic and copies ran while one was open for 4% of the time, Pallas kernels for 0%

commit v1 on v0

v1 whole, which is shorter than its diff:
```python
import jax
import jax.numpy as jnp
from jax import lax
from jax.experimental import pallas as pl
from jax.experimental.pallas import tpu as pltpu
from jax.sharding import PartitionSpec as P

HD = 64
BLK = 128
F32 = jnp.float32
BF = jnp.bfloat16
NT = (((1,), (1,)), ((), ()))
NN = (((1,), (0,)), ((), ()))


def mm(a, b, dims=NN):
    return lax.dot_general(a, b, dims, preferred_element_type=F32)


def heads_side(x, lane):
    zero = jnp.zeros_like(x)
    return jnp.concatenate([jnp.where(lane < HD, x, zero), jnp.where(lane < HD, zero, x)], axis=0)


def heads_rows(xt, row):
    zero = jnp.zeros_like(xt)
    return jnp.concatenate([jnp.where(row < HD, xt, zero), jnp.where(row < HD, zero, xt)], axis=1)


def fwd_kernel(bias_ref, q_ref, kb_ref, ko_ref, ka_ref, vb_ref, vo_ref, va_ref, og_ref,
               expo_ref, sum_ref, att_ref, wterm_ref, s_ref):
    tok = q_ref.shape[0]
    nblk = tok // BLK
    lane = lax.broadcasted_iota(jnp.int32, (tok, 2 * HD), 1)
    row = lax.broadcasted_iota(jnp.int32, (2 * HD, tok), 0)
    q = q_ref[...] * jnp.asarray(0.125, BF)
    qcat = heads_side(q, lane)
    top = None
    for t, k_ref in enumerate((kb_ref, ko_ref, ka_ref)):
        s = mm(k_ref[...], qcat, NT)
        for j in range(nblk):
            w = t * nblk + j
            part = s[j * BLK:(j + 1) * BLK] + bias_ref[w:w + 1, :]
            s_ref[w * BLK:(w + 1) * BLK, :] = part
            peak = jnp.max(part.reshape(BLK // 8, 8, 2 * tok), axis=0)
            top = peak if top is None else jnp.maximum(top, peak)
    top = jnp.max(top, axis=0, keepdims=True)
    total = jnp.zeros((8, 2 * tok), F32)
    acc = jnp.zeros((2 * HD, 2 * tok), F32)
    for t, v_ref in enumerate((vb_ref, vo_ref, va_ref)):
        e = jnp.exp(s_ref[t * tok:(t + 1) * tok, :] - top)
        total += jnp.sum(e.reshape(tok // 8, 8, 2 * tok), axis=0)
        eh = e.astype(BF)
        expo_ref[t * tok:(t + 1) * tok, :] = eh
        acc += mm(v_ref[...].T, eh)
    inv = 1.0 / jnp.sum(total, axis=0, keepdims=True)
    acc = acc * inv
    att = jnp.where(row < HD, acc[:, :tok], acc[:, tok:]).astype(BF)
    sum_ref[...] = inv
    att_ref[...] = att
    wterm_ref[...] = mm(att, og_ref[...]).astype(wterm_ref.dtype)


def bwd_kernel(q_ref, kb_ref, ko_ref, ka_ref, vb_ref, vo_ref, va_ref, og_ref, w_ref,
               expo_ref, sum_ref, att_ref,
               dq_ref, dkb_ref, dko_ref, dka_ref, dvb_ref, dvo_ref, dva_ref):
    tok = q_ref.shape[0]
    lane = lax.broadcasted_iota(jnp.int32, (tok, 2 * HD), 1)
    row = lax.broadcasted_iota(jnp.int32, (2 * HD, tok), 0)
    inv = sum_ref[...]
    qcat = heads_side(q_ref[...] * jnp.asarray(0.125, BF), lane)
    do_t = mm(w_ref[...], og_ref[...], NT).astype(BF)
    do_f = do_t.astype(F32)
    prod = do_f * att_ref[...].astype(F32)
    delta = jnp.concatenate([jnp.sum(prod[:HD], axis=0, keepdims=True),
                             jnp.sum(prod[HD:], axis=0, keepdims=True)], axis=1) * inv
    do_rows = (heads_rows(do_f, row) * inv).astype(BF)
    do_side = do_rows.T
    dq = jnp.zeros((2 * HD, 2 * tok), F32)
    for t, (k_ref, v_ref, dk_ref, dv_ref) in enumerate((
            (kb_ref, vb_ref, dkb_ref, dvb_ref), (ko_ref, vo_ref, dko_ref, dvo_ref),
            (ka_ref, va_ref, dka_ref, dva_ref))):
        eh = expo_ref[t * tok:(t + 1) * tok, :]
        dp = mm(v_ref[...], do_rows)
        ds = (eh.astype(F32) * (dp - delta)).astype(BF)
        dv_ref[...] = mm(eh, do_side).astype(dv_ref.dtype)
        dk_ref[...] = mm(ds, qcat).astype(dk_ref.dtype)
        dq += mm(k_ref[...].T, ds)
    dq = jnp.where(row < HD, dq[:, :tok], dq[:, tok:]) * 0.125
    dq_ref[...] = dq.T.astype(dq_ref.dtype)


def col(tok):
    return pl.BlockSpec((tok, 2 * HD), lambda p: (0, p))


def forward(bias, q, kb, ko, ka, vb, vo, va, og):
    tok, width = q.shape
    pairs = width // (2 * HD)
    c = col(tok)
    full = lambda a: pl.BlockSpec(a.shape, lambda p: (0, 0))
    return pl.pallas_call(
        fwd_kernel,
        grid=(pairs,),
        in_specs=[full(bias), c, c, c, c, c, c, c, full(og)],
        out_specs=[
            pl.BlockSpec((None, 3 * tok, 2 * tok), lambda p: (p, 0, 0)),
            pl.BlockSpec((None, 1, 2 * tok), lambda p: (p, 0, 0)),
            pl.BlockSpec((2 * HD, tok), lambda p: (p, 0)),
            pl.BlockSpec((2 * HD, width), lambda p: (p, 0)),
        ],
        out_shape=[
            jax.ShapeDtypeStruct((pairs, 3 * tok, 2 * tok), BF),
            jax.ShapeDtypeStruct((pairs, 1, 2 * tok), F32),
            jax.ShapeDtypeStruct((width, tok), BF),
            jax.ShapeDtypeStruct((width, width), BF),
        ],
        scratch_shapes=[pltpu.VMEM((3 * tok, 2 * tok), F32)],
        cost_estimate=pl.CostEstimate(flops=4 * 3 * tok * tok * width, bytes_accessed=16 << 20, transcendentals=3 * tok * tok * width // HD),
        name="fwd",
    )(bias, q, kb, ko, ka, vb, vo, va, og)


def backward(q, kb, ko, ka, vb, vo, va, og, w, expo, inv, att):
    tok, width = q.shape
    pairs = width // (2 * HD)
    c = col(tok)
    full = lambda a: pl.BlockSpec(a.shape, lambda p: (0, 0))
    half = jax.ShapeDtypeStruct((tok, width), BF)
    wide = jax.ShapeDtypeStruct((tok, width), F32)
    return pl.pallas_call(
        bwd_kernel,
        grid=(pairs,),
        in_specs=[c, c, c, c, c, c, c, full(og), pl.BlockSpec((2 * HD, width), lambda p: (p, 0)),
            pl.BlockSpec((None, 3 * tok, 2 * tok), lambda p: (p, 0, 0)),
            pl.BlockSpec((None, 1, 2 * tok), lambda p: (p, 0, 0)),
            pl.BlockSpec((2 * HD, tok), lambda p: (p, 0)),
        ],
        out_specs=[c] * 7,
        out_shape=[half, half, wide, half, half, wide, half],
        cost_estimate=pl.CostEstimate(flops=8 * 3 * tok * tok * width, bytes_accessed=20 << 20, transcendentals=0),
        name="bwd",
    )(q, kb, ko, ka, vb, vo, va, og, w, expo, inv, att)


def shifted(block, distance):
    count = lax.axis_size("space")
    return lax.ppermute(block, "space", [((i - distance) % count, i) for i in range(count)])


def block_bias(neighbours, live_count, tokens):
    nblock, slots = neighbours.shape
    total = nblock * lax.axis_size("space")
    ids = jnp.mod(neighbours - (lax.axis_index("space") - 1) * nblock, total)
    used = jnp.arange(slots)[None, :] < live_count[:, None]
    names = ids[None] == jnp.arange(3 * nblock)[:, None, None]
    live = jnp.any(names & used[None], axis=-1)
    bias = jnp.where(live, 0.0, -1e30).astype(F32)
    wide = jnp.broadcast_to(bias[:, None, :, None], (3 * nblock, 2, nblock, BLK))
    return wide.reshape(3 * nblock, 2 * tokens)


def body(queries, keys, values, out_grad, w_out, neighbours, live_count):
    q, k, v, og = queries[0], keys[0], values[0], out_grad[0]
    tokens, width = q.shape
    kb, ka = shifted(k, 1), shifted(k, -1)
    vb, va = shifted(v, 1), shifted(v, -1)
    w = lax.all_gather(w_out, "dp", axis=0, tiled=True)
    bias = block_bias(neighbours, live_count, tokens)
    expo, inv, att, wterm = forward(bias, q, kb, k, ka, vb, v, va, og)
    rows = width // lax.axis_size("dp")
    whole = lax.psum(wterm, ("dp", "space"))
    weight_grad = lax.dynamic_slice_in_dim(whole, lax.axis_index("dp") * rows, rows, 0).astype(F32)
    dq, dkb, dko, dka, dvb, dvo, dva = backward(q, kb, k, ka, vb, v, va, og, w, expo, inv, att)

    def total(own, upper, lower):
        return (own + shifted(upper, 1).astype(F32) + shifted(lower, -1).astype(F32)).astype(BF)

    dk = total(dko, dka, dkb)
    dv = total(dvo, dva, dvb)
    return (dq[None], dk[None], dv[None], weight_grad)


def solution(mesh):
    rows = P("dp", "space", None)
    return jax.shard_map(
        body,
        mesh=mesh,
        in_specs=(rows, rows, rows, rows, P("dp", None), P("space", None), P("space")),
        out_specs=(rows, rows, rows, P("dp", None)),
        check_vma=False,
    )
```

time: 1080 us -> 574 us (0.53)
  blocking collectives: 423 us -> 0 us
  waiting for transfers between devices: 166 us -> 457 us
  local copies, waits for them, and re-layouts: 213 us -> 1.54 us
  other arithmetic: 134 us -> 6.71 us
  matrix products: 72.8 us -> 0 us
  Pallas kernels: 0 us -> 32.1 us
  starting transfers between devices: 31.3 us -> 59.9 us
  loops' own time: 19 us -> 0 us
    psum x1 -> x0, blocking collectives: 423 us -> none  [body(): weight_grad = lax.psum(reduced, 'space')]
    psum x0 -> x1, waiting for transfers between devices: none -> 397 us  [body(): whole = lax.psum(wterm, ('dp', 'space'))]
    scatter-add x9 -> x0, other arithmetic: 72.5 us -> none  [step_fn(): carry = carry.at[group, ids].add(terms)]
    dynamic_slice x45 -> x0, local copies, waits for them, and re-layouts: 50.4 us -> none  [the longest x18 14.2 us: step_fn(): lax.dynamic_slice(d_attended, (block * BLK, column), (BLK, group_width))]
    reshape x21 -> x1, local copies, waits for them, and re-layouts: 50.6 us -> 0.65 us  [block_bias(): return wide.reshape(3 * nblock, 2 * tokens)]
    dot_general x47 -> x0, matrix products: 44.7 us -> none  [the longest x9 12.8 us: step_fn(): jnp.einsum('hqk,qhd->khd', dscores, query_heads, preferred_element_type=j...]
    reduce_scatter x1 -> x0, waiting for transfers between devices: 43.2 us -> none  [body(): lax.psum_scatter(weight_term.astype(jnp.bfloat16), 'dp', scatter_dimensio...]
    ppermute x4 -> x8, waiting for transfers between devices: 60.4 us -> 19.8 us  [shifted(): lax.ppermute(block, 'space', [((i - distance) % count, i) for i in range(...]
  transfers between devices with their start and end apart: 6 -> 10, of which waited for: 5 -> 5; matrix products, arithmetic and copies ran while one was open for 4% -> 1% of each run, Pallas kernels for 0% -> 6%
where the time goes in v1:
time: 574 us; the launch traced here: 573 us
  waiting for transfers between devices  457 us (80%)
  starting transfers between devices  59.9 us (10%)
  Pallas kernels  32.1 us (6%)
  between operations  15.6 us (3%)
  other arithmetic  6.71 us (1%)
    psum x1, waiting for transfers between devices, body(): whole = lax.psum(wterm, ('dp', 'space'))  397 us
    ppermute x8, starting transfers between devices, shifted(): lax.ppermute(block, 'space', [((i - distance) % count, i) for i in range(...  59.8 us
    all_gather x1, waiting for transfers between devices, body(): w = lax.all_gather(w_out, 'dp', axis=0, tiled=True)  39.9 us
    ppermute x8, waiting for transfers between devices, shifted(): lax.ppermute(block, 'space', [((i - distance) % count, i) for i in range(...  19.8 us
    pallas_call x1, Pallas kernels, backward(): pl.pallas_call(bwd_kernel, grid=(pairs,), in_specs=[c, c, c, c, c, c, c,...  17.2 us
    pallas_call x1, Pallas kernels, forward(): pl.pallas_call(fwd_kernel, grid=(pairs,), in_specs=[full(bias), c, c, c,...  14.9 us
  transfers between devices with their start and end apart: 10, of which 5 were waited for; matrix products, arithmetic and copies ran while one was open for 1% of the time, Pallas kernels for 6%

profile of v1, /device:TPU:6, one launch (start us, length us, event | category | flops | bytes accessed | tf_op | source)
XLA Modules:
  0.0 573.3 jit_solution(2469599912196027732)
XLA Ops:
  8.0 0.0 all-gather.2.cloned.1.call-start
  8.0 0.7 all-gather.2.cloned.1.call-update
  8.7 0.0 all-reduce.2.cloned.1.call-start
  8.8 15.1 %collective-permute-start.1 = (bf16[384,768]{1,0:T(8,128)(2,1)}, bf16[384,768]{1,0:T(8,128)(2,1)S(1)}, u32[]{:S(2)}, u32[]{:S(2)}) collective-permute-start(bf16[384,768]{1,0:T(8,128)(2,1)} %bitcast.11), channel_id=1, source_target_pairs={{1,0},{2,1},{3,2},{4,3},{5,4},{6,5},{7,6},{8,7},{9,8},{10,9},{11,1... | collective-permute-start | bytes 1769480 | tf_op jit(solution)/shard_map/ppermute | solution.py:148
  23.8 1.9 collective-permute-start
  25.8 12.4 %collective-permute-start.3 = (bf16[384,768]{1,0:T(8,128)(2,1)}, bf16[384,768]{1,0:T(8,128)(2,1)S(1)}, u32[]{:S(2)}, u32[]{:S(2)}) collective-permute-start(bf16[384,768]{1,0:T(8,128)(2,1)} %bitcast.15), channel_id=1, source_target_pairs={{1,0},{2,1},{3,2},{4,3},{5,4},{6,5},{7,6},{8,7},{9,8},{10,9},{11,1... | collective-permute-start | bytes 1769480 | tf_op jit(solution)/shard_map/ppermute | solution.py:148
  38.1 1.9 collective-permute-start.2
  40.1 0.7 iota_compare_fusion.1
  40.8 0.7 add_select_fusion
  41.5 0.3 fusion.3
  41.8 0.1 broadcast_in_dim.30
  41.8 0.7 reshape.33.bias_ref
  42.5 0.0 collective-permute-done.1.ka_ref
  42.5 2.9 collective-permute-done.kb_ref
  45.4 5.1 collective-permute-done.3.va_ref
  50.5 11.7 %collective-permute-done.2.vb_ref = bf16[384,768]{1,0:T(8,128)(2,1)S(1)} collective-permute-done((bf16[384,768]{1,0:T(8,128)(2,1)}, bf16[384,768]{1,0:T(8,128)(2,1)S(1)}, u32[]{:S(2)}, u32[]{:S(2)}) %collective-permute-start.2) | collective-permute-done | bytes 589856 | tf_op jit(solution)/shard_map/ppermute | solution.py:148
  62.3 0.8 copy-done.4
  63.1 14.9 %fwd.1 = (bf16[6,1152,768]{2,1,0:T(8,128)(2,1)}, f32[6,1,768]{2,1,0:T(1,128)}, bf16[768,384]{1,0:T(8,128)(2,1)}, bf16[768,768]{1,0:T(8,128)(2,1)}) custom-call(f32[9,768]{1,0:T(8,128)} %reshape.33.bias_ref, bf16[384,768]{1,0:T(8,128)(2,1)} %bitcast.9, bf16[384,768]{1,0:T(8,128)(2,1)} %copy-done.2, bf16[384,768]{1,0:T(8,128)(2,1)} %bitcast.13, ...), custom_call_target="tpu_custom_call" | custom-call | flops 1358954496 | bytes 16777216 | tf_op jit(solution)/shard_map/fwd/pallas_call | solution.py:102
  77.9 0.0 all-reduce.2.cloned.1.call-update
  78.0 39.9 %all-gather.2.cloned.1.call-done.w_ref = bf16[768,768]{1,0:T(8,128)(2,1)} async-done(((bf16[96,768]{1,0:T(8,128)(2,1)}), bf16[768,768]{1,0:T(8,128)(2,1)}) %all-gather.2.cloned.1.call-update) | async-done | bytes 1179664 | tf_op jit(solution)/shard_map/all_gather | solution.py:168
  117.8 17.2 %bwd.1 = (bf16[384,768]{1,0:T(8,128)(2,1)}, bf16[384,768]{1,0:T(8,128)(2,1)}, f32[384,768]{1,0:T(8,128)}, bf16[384,768]{1,0:T(8,128)(2,1)}, bf16[384,768]{1,0:T(...) custom-call(bf16[384,768]{1,0:T(8,128)(2,1)} %bitcast.10, bf16[384,768]{1,0:T(8,128)(2,1)} %copy-done.2, ...), custom_call_target="tpu_custom_call" | custom-call | flops 2717908992 | bytes 20971520 | tf_op jit(solution)/shard_map/bwd/pallas_call | solution.py:131
  135.0 1.9 collective-permute-start.4
  137.0 12.4 %collective-permute-start.5 = (bf16[384,768]{1,0:T(8,128)(2,1)}, bf16[384,768]{1,0:T(8,128)(2,1)S(1)}, u32[]{:S(2)}, u32[]{:S(2)}) collective-permute-start(bf16[384,768]{1,0:T(8,128)(2,1)} %get-tuple-element.21), channel_id=1, source_target_pairs={{1,0},{2,1},{3,2},{4,3},{5,4},{6,5},{7,6},{8,7},{9,8},{10,9},{11,1... | collective-permute-start | bytes 1769480 | tf_op jit(solution)/shard_map/ppermute | solution.py:148
  149.3 1.9 collective-permute-start.6
  151.2 12.4 %collective-permute-start.7 = (bf16[384,768]{1,0:T(8,128)(2,1)}, bf16[384,768]{1,0:T(8,128)(2,1)S(1)}, u32[]{:S(2)}, u32[]{:S(2)}) collective-permute-start(bf16[384,768]{1,0:T(8,128)(2,1)} %get-tuple-element.24), channel_id=1, source_target_pairs={{1,0},{2,1},{3,2},{4,3},{5,4},{6,5},{7,6},{8,7},{9,8},{10,9},{11,1... | collective-permute-start | bytes 1769480 | tf_op jit(solution)/shard_map/ppermute | solution.py:148
  163.6 397.2 %all-reduce.2.cloned.1.call-done = bf16[768,768]{1,0:T(8,128)(2,1)} async-done(((bf16[768,768]{1,0:T(8,128)(2,1)}), bf16[768,768]{1,0:T(8,128)(2,1)}) %all-reduce.2.cloned.1.call-update) | async-done | bytes 1179664 | tf_op jit(solution)/shard_map/psum | solution.py:172
  560.8 1.6 dynamic-slice_convert_fusion
  562.4 0.0 collective-permute-done.4
  562.4 0.0 collective-permute-done.5
  562.4 2.4 fusion
  564.8 0.0 collective-permute-done.7
  564.8 1.0 fusion.1
  (11 shorter events, 0.0 us)
Async XLA Ops:
  8.0 109.8 %all-gather.2.cloned.1.call-start = ((), (), s32[]{:S(2)}) async-start(), calls=%async_computation | async-start | bytes 1327104 | tf_op jit(solution)/shard_map/all_gather | solution.py:168
  8.7 552.1 %all-reduce.2.cloned.1.call-start = ((), (), s32[]{:S(2)}) async-start(), calls=%async_computation.1 | async-start | bytes 2359296 | tf_op jit(solution)/shard_map/psum | solution.py:172
  8.8 33.7 %collective-permute-start.1 = (bf16[384,768]{1,0:T(8,128)(2,1)}, bf16[384,768]{1,0:T(8,128)(2,1)S(1)}, u32[]{:S(2)}, u32[]{:S(2)}) collective-permute-start(bf16[384,768]{1,0:T(8,128)(2,1)} %bitcast.11), channel_id=1, source_target_pairs={{1,0},{2,1},{3,2},{4,3},{5,4},{6,5},{7,6},{8,7},{9,8},{10,9},{11,1... | collective-permute-start | bytes 1769480 | tf_op jit(solution)/shard_map/ppermute | solution.py:148
  23.8 21.6 %collective-permute-start = (bf16[384,768]{1,0:T(8,128)(2,1)}, bf16[384,768]{1,0:T(8,128)(2,1)S(1)}, u32[]{:S(2)}, u32[]{:S(2)}) collective-permute-start(bf16[384,768]{1,0:T(8,128)(2,1)} %bitcast.12), channel_id=1, source_target_pairs={{63,0},{0,1},{1,2},{2,3},{3,4},{4,5},{5,6},{6,7},{7,8},{8,9},{9,10... | collective-permute-start | bytes 1769480 | tf_op jit(solution)/shard_map/ppermute | solution.py:148
  25.8 24.8 %collective-permute-start.3 = (bf16[384,768]{1,0:T(8,128)(2,1)}, bf16[384,768]{1,0:T(8,128)(2,1)S(1)}, u32[]{:S(2)}, u32[]{:S(2)}) collective-permute-start(bf16[384,768]{1,0:T(8,128)(2,1)} %bitcast.15), channel_id=1, source_target_pairs={{1,0},{2,1},{3,2},{4,3},{5,4},{6,5},{7,6},{8,7},{9,8},{10,9},{11,1... | collective-permute-start | bytes 1769480 | tf_op jit(solution)/shard_map/ppermute | solution.py:148
  38.1 24.1 %collective-permute-start.2 = (bf16[384,768]{1,0:T(8,128)(2,1)}, bf16[384,768]{1,0:T(8,128)(2,1)S(1)}, u32[]{:S(2)}, u32[]{:S(2)}) collective-permute-start(bf16[384,768]{1,0:T(8,128)(2,1)} %bitcast.16), channel_id=1, source_target_pairs={{63,0},{0,1},{1,2},{2,3},{3,4},{4,5},{5,6},{6,7},{7,8},{8,9},{9,10... | collective-permute-start | bytes 1769480 | tf_op jit(solution)/shard_map/ppermute | solution.py:148
  42.5 19.8 %copy-start.1 = (bf16[384,768]{1,0:T(8,128)(2,1)}, bf16[384,768]{1,0:T(8,128)(2,1)S(1)}, u32[]{:S(2)}) copy-start(bf16[384,768]{1,0:T(8,128)(2,1)S(1)} %collective-permute-done.1.ka_ref) | copy-start | bytes 1769476
  45.4 16.9 %copy-start.2 = (bf16[384,768]{1,0:T(8,128)(2,1)}, bf16[384,768]{1,0:T(8,128)(2,1)S(1)}, u32[]{:S(2)}) copy-start(bf16[384,768]{1,0:T(8,128)(2,1)S(1)} %collective-permute-done.kb_ref) | copy-start | bytes 1769476
  50.5 11.7 %copy-start.3 = (bf16[384,768]{1,0:T(8,128)(2,1)}, bf16[384,768]{1,0:T(8,128)(2,1)S(1)}, u32[]{:S(2)}) copy-start(bf16[384,768]{1,0:T(8,128)(2,1)S(1)} %collective-permute-done.3.va_ref) | copy-start | bytes 1769476
  62.2 0.8 copy-start.4
  135.0 427.4 %collective-permute-start.4 = (bf16[384,768]{1,0:T(8,128)(2,1)}, bf16[384,768]{1,0:T(8,128)(2,1)S(1)}, u32[]{:S(2)}, u32[]{:S(2)}) collective-permute-start(bf16[384,768]{1,0:T(8,128)(2,1)} %get-tuple-element.20), channel_id=1, source_target_pairs={{63,0},{0,1},{1,2},{2,3},{3,4},{4,5},{5,6},{6,7},{7,8},{8,9},{9,10... | collective-permute-start | bytes 1769480 | tf_op jit(solution)/shard_map/ppermute | solution.py:148
  137.0 425.5 %collective-permute-start.5 = (bf16[384,768]{1,0:T(8,128)(2,1)}, bf16[384,768]{1,0:T(8,128)(2,1)S(1)}, u32[]{:S(2)}, u32[]{:S(2)}) collective-permute-start(bf16[384,768]{1,0:T(8,128)(2,1)} %get-tuple-element.21), channel_id=1, source_target_pairs={{1,0},{2,1},{3,2},{4,3},{5,4},{6,5},{7,6},{8,7},{9,8},{10,9},{11,1... | collective-permute-start | bytes 1769480 | tf_op jit(solution)/shard_map/ppermute | solution.py:148
  149.3 415.5 %collective-permute-start.6 = (bf16[384,768]{1,0:T(8,128)(2,1)}, bf16[384,768]{1,0:T(8,128)(2,1)S(1)}, u32[]{:S(2)}, u32[]{:S(2)}) collective-permute-start(bf16[384,768]{1,0:T(8,128)(2,1)} %get-tuple-element.23), channel_id=1, source_target_pairs={{63,0},{0,1},{1,2},{2,3},{3,4},{4,5},{5,6},{6,7},{7,8},{8,9},{9,10... | collective-permute-start | bytes 1769480 | tf_op jit(solution)/shard_map/ppermute | solution.py:148
  151.2 413.6 %collective-permute-start.7 = (bf16[384,768]{1,0:T(8,128)(2,1)}, bf16[384,768]{1,0:T(8,128)(2,1)S(1)}, u32[]{:S(2)}, u32[]{:S(2)}) collective-permute-start(bf16[384,768]{1,0:T(8,128)(2,1)} %get-tuple-element.24), channel_id=1, source_target_pairs={{1,0},{2,1},{3,2},{4,3},{5,4},{6,5},{7,6},{8,7},{9,8},{10,9},{11,1... | collective-permute-start | bytes 1769480 | tf_op jit(solution)/shard_map/ppermute | solution.py:148
  562.4 2.4 copy-start
Sparse Core Ops, SparseCore 0:
  12.0 105.7 all-gather.1
Sparse Core Ops, SparseCore 1:
  78.0 482.7 all-reduce.1

commit v2 on v1

--- a/solution.py
+++ b/solution.py
@@ -58,18 +58,36 @@
     att = jnp.where(row < HD, acc[:, :tok], acc[:, tok:]).astype(BF)
     sum_ref[...] = inv
     att_ref[...] = att
-    wterm_ref[...] = mm(att, og_ref[...]).astype(wterm_ref.dtype)
-
-
-def bwd_kernel(q_ref, kb_ref, ko_ref, ka_ref, vb_ref, vo_ref, va_ref, og_ref, w_ref,
+    wterm = mm(att, og_ref[...]).astype(wterm_ref.dtype)
+    wide = wterm_ref.shape[2]
+    wterm_ref[0] = wterm[:, :wide]
+    wterm_ref[1] = wterm[:, wide:]
+
+
+def bwd_kernel(place_ref, q_ref, kb_ref, ko_ref, ka_ref, vb_ref, vo_ref, va_ref, og_ref, w_ref, wx_ref,
                expo_ref, sum_ref, att_ref,
-               dq_ref, dkb_ref, dko_ref, dka_ref, dvb_ref, dvo_ref, dva_ref):
+               dq_ref, dkb_ref, dko_ref, dka_ref, dvb_ref, dvo_ref, dva_ref, do_ref):
     tok = q_ref.shape[0]
     lane = lax.broadcasted_iota(jnp.int32, (tok, 2 * HD), 1)
     row = lax.broadcasted_iota(jnp.int32, (2 * HD, tok), 0)
     inv = sum_ref[...]
     qcat = heads_side(q_ref[...] * jnp.asarray(0.125, BF), lane)
-    do_t = mm(w_ref[...], og_ref[...], NT).astype(BF)
+    pair = pl.program_id(0)
+
+    @pl.when(pair == 0)
+    def _():
+        shards = place_ref.shape[0] - 1
+        rows = w_ref.shape[0] // shards
+        wide = w_ref.shape[1]
+        mine = place_ref[shards]
+        og_mine = og_ref[:, pl.ds(pl.multiple_of(mine * wide, wide), wide)]
+        og_other = og_ref[:, pl.ds(pl.multiple_of((1 - mine) * wide, wide), wide)]
+        for r in range(shards):
+            span = slice(r * rows, (r + 1) * rows)
+            part = mm(w_ref[span, :], og_mine, NT) + mm(wx_ref[span, :], og_other, NT)
+            do_ref[pl.ds(pl.multiple_of(place_ref[r] * rows, rows), rows), :] = part.astype(BF)
+
+    do_t = do_ref[pl.ds(pl.multiple_of(pair * 2 * HD, 2 * HD), 2 * HD), :]
     do_f = do_t.astype(F32)
     prod = do_f * att_ref[...].astype(F32)
     delta = jnp.concatenate([jnp.sum(prod[:HD], axis=0, keepdims=True),
@@ -107,13 +125,13 @@
             pl.BlockSpec((None, 3 * tok, 2 * tok), lambda p: (p, 0, 0)),
             pl.BlockSpec((None, 1, 2 * tok), lambda p: (p, 0, 0)),
             pl.BlockSpec((2 * HD, tok), lambda p: (p, 0)),
-            pl.BlockSpec((2 * HD, width), lambda p: (p, 0)),
+            pl.BlockSpec((2, 2 * HD, width // 2), lambda p: (0, p, 0)),
         ],
         out_shape=[
             jax.ShapeDtypeStruct((pairs, 3 * tok, 2 * tok), BF),
             jax.ShapeDtypeStruct((pairs, 1, 2 * tok), F32),
             jax.ShapeDtypeStruct((width, tok), BF),
-            jax.ShapeDtypeStruct((width, width), BF),
+            jax.ShapeDtypeStruct((2, width, width // 2), BF),
         ],
         scratch_shapes=[pltpu.VMEM((3 * tok, 2 * tok), F32)],
         cost_estimate=pl.CostEstimate(flops=4 * 3 * tok * tok * width, bytes_accessed=16 << 20, transcendentals=3 * tok * tok * width // HD),
@@ -121,7 +139,7 @@
     )(bias, q, kb, ko, ka, vb, vo, va, og)
 
 
-def backward(q, kb, ko, ka, vb, vo, va, og, w, expo, inv, att):
+def backward(place, q, kb, ko, ka, vb, vo, va, og, w, wx, expo, inv, att):
     tok, width = q.shape
     pairs = width // (2 * HD)
     c = col(tok)
@@ -131,21 +149,84 @@
     return pl.pallas_call(
         bwd_kernel,
         grid=(pairs,),
-        in_specs=[c, c, c, c, c, c, c, full(og), pl.BlockSpec((2 * HD, width), lambda p: (p, 0)),
+        in_specs=[pl.BlockSpec(memory_space=pltpu.SMEM), c, c, c, c, c, c, c, full(og), full(w), full(wx),
             pl.BlockSpec((None, 3 * tok, 2 * tok), lambda p: (p, 0, 0)),
             pl.BlockSpec((None, 1, 2 * tok), lambda p: (p, 0, 0)),
             pl.BlockSpec((2 * HD, tok), lambda p: (p, 0)),
         ],
         out_specs=[c] * 7,
         out_shape=[half, half, wide, half, half, wide, half],
+        scratch_shapes=[pltpu.VMEM((width, tok), BF)],
         cost_estimate=pl.CostEstimate(flops=8 * 3 * tok * tok * width, bytes_accessed=20 << 20, transcendentals=0),
         name="bwd",
-    )(q, kb, ko, ka, vb, vo, va, og, w, expo, inv, att)
+    )(place, q, kb, ko, ka, vb, vo, va, og, w, wx, expo, inv, att)
+
+
+def move(block, axis, target):
+    return lax.ppermute(block, axis, [(i, target(i)) for i in range(lax.axis_size(axis))])
 
 
 def shifted(block, distance):
     count = lax.axis_size("space")
-    return lax.ppermute(block, "space", [((i - distance) % count, i) for i in range(count)])
+    return move(block, "space", lambda i: (i + distance) % count)
+
+
+def core_swap(block):
+    return move(block, "space", lambda i: i ^ 1)
+
+
+def along_y(block, distance):
+    return move(block, "space", lambda i: (i & 15) | ((((i >> 4) + distance) & 3) << 4))
+
+
+def along_x(block, distance):
+    return move(block, "dp", lambda i: (i & 4) | ((i + distance) & 3))
+
+
+def far_swap(block):
+    return move(block, "dp", lambda i: i ^ 4)
+
+
+def add_up(*terms):
+    total = terms[0].astype(F32)
+    for term in terms[1:]:
+        total = total + term.astype(F32)
+    return lax.optimization_barrier(total.astype(BF))
+
+
+def pick(array, index, axis):
+    return lax.dynamic_index_in_dim(array, index, axis, keepdims=False)
+
+
+def gather_weight(w_out):
+    dp, space = lax.axis_index("dp"), lax.axis_index("space")
+    half = w_out.shape[1] // 2
+    near = lax.dynamic_slice_in_dim(w_out, (space & 1) * half, half, 1)
+    far = far_swap(near)
+    blocks = [near, *(along_x(near, d) for d in (1, 2, 3)), far, *(along_x(far, d) for d in (1, 2, 3))]
+    mine = jnp.concatenate(blocks, axis=0)
+    places = [((dp & 4) ^ (4 * f)) | ((dp - d) & 3) for f in (0, 1) for d in range(4)]
+    return mine, core_swap(mine), jnp.stack([*places, space & 1]).astype(jnp.int32)
+
+
+def sum_weight(wterm):
+    dp, space = lax.axis_index("dp"), lax.axis_index("space")
+    far, x, y, core = dp >> 2, dp & 3, space >> 4, space & 1
+    rows, half = wterm.shape[1] // 8, wterm.shape[2]
+    part = add_up(pick(wterm, core, 0), core_swap(pick(wterm, 1 - core, 0)))
+    part = part.reshape(2, 4, rows, half)
+    part = add_up(pick(part, x, 1), *(along_x(pick(part, (x + d) & 3, 1), d) for d in (1, 2, 3)))
+    part = part.reshape(2, 4, rows // 4, half)
+    part = add_up(pick(part, y, 1), *(along_y(pick(part, (y + d) & 3, 1), d) for d in (1, 2, 3)))
+    part = add_up(pick(part, far, 0), far_swap(pick(part, 1 - far, 0)))
+    for bit in (2, 4, 8):
+        part = add_up(part, move(part, "space", lambda i: i ^ bit))
+    ring = jnp.stack([part, *(along_y(part, d) for d in (3, 2, 1))])
+    ring = jnp.concatenate([ring, ring], axis=0)
+    mine = lax.dynamic_slice_in_dim(ring, (-y) & 3, 4, 0).reshape(rows, half)
+    other = core_swap(mine)
+    pair = jnp.where(core == 0, jnp.concatenate([mine, other], axis=1), jnp.concatenate([other, mine], axis=1))
+    return pair.astype(F32)
 
 
 def block_bias(neighbours, live_count, tokens):
@@ -162,16 +243,14 @@
 
 def body(queries, keys, values, out_grad, w_out, neighbours, live_count):
     q, k, v, og = queries[0], keys[0], values[0], out_grad[0]
-    tokens, width = q.shape
+    tokens = q.shape[0]
     kb, ka = shifted(k, 1), shifted(k, -1)
     vb, va = shifted(v, 1), shifted(v, -1)
-    w = lax.all_gather(w_out, "dp", axis=0, tiled=True)
+    w, wx, place = gather_weight(w_out)
     bias = block_bias(neighbours, live_count, tokens)
     expo, inv, att, wterm = forward(bias, q, kb, k, ka, vb, v, va, og)
-    rows = width // lax.axis_size("dp")
-    whole = lax.psum(wterm, ("dp", "space"))
-    weight_grad = lax.dynamic_slice_in_dim(whole, lax.axis_index("dp") * rows, rows, 0).astype(F32)
-    dq, dkb, dko, dka, dvb, dvo, dva = backward(q, kb, k, ka, vb, v, va, og, w, expo, inv, att)
+    weight_grad = sum_weight(wterm)
+    dq, dkb, dko, dka, dvb, dvo, dva = backward(place, q, kb, k, ka, vb, v, va, og, w, wx, expo, inv, att)
 
     def total(own, upper, lower):
         return (own + shifted(upper, 1).astype(F32) + shifted(lower, -1).astype(F32)).astype(BF)

time: 574 us -> 214 us (0.37)
  waiting for transfers between devices: 457 us -> 23.7 us
  starting transfers between devices: 59.9 us -> 141 us
  between operations: 15.6 us -> 1.31 us
  local copies, waits for them, and re-layouts: 1.54 us -> 8.15 us
    psum x1 -> x0, waiting for transfers between devices: 397 us -> none  [body(): whole = lax.psum(wterm, ('dp', 'space'))]
    ppermute x8 -> x31, starting transfers between devices: 59.8 us -> 141 us  [move(): lax.ppermute(block, axis, [(i, target(i)) for i in range(lax.axis_size(ax...]
    all_gather x1 -> x0, waiting for transfers between devices: 39.9 us -> none  [body(): w = lax.all_gather(w_out, 'dp', axis=0, tiled=True)]
    ppermute x8 -> x31, waiting for transfers between devices: 19.8 us -> 23.7 us  [move(): lax.ppermute(block, axis, [(i, target(i)) for i in range(lax.axis_size(ax...]
  transfers between devices with their start and end apart: 10 -> 31, of which waited for: 5 -> 8; matrix products, arithmetic and copies ran while one was open for 1% -> 5% of each run, Pallas kernels for 6% -> 15%
where the time goes in v2:
time: 214 us; the launch traced here: 212 us
  starting transfers between devices  141 us (66%)
  Pallas kernels  32.4 us (15%)
  waiting for transfers between devices  23.7 us (11%)
  local copies, waits for them, and re-layouts  8.15 us (4%)
  other arithmetic  6.08 us (3%)
    ppermute x31, starting transfers between devices, move(): lax.ppermute(block, axis, [(i, target(i)) for i in range(lax.axis_size(ax...  141 us
    ppermute x31, waiting for transfers between devices, move(): lax.ppermute(block, axis, [(i, target(i)) for i in range(lax.axis_size(ax...  23.7 us
    pallas_call x1, Pallas kernels, backward(): pl.pallas_call(bwd_kernel, grid=(pairs,), in_specs=[pl.BlockSpec(memory_s...  17.5 us
    pallas_call x1, Pallas kernels, forward(): pl.pallas_call(fwd_kernel, grid=(pairs,), in_specs=[full(bias), c, c, c,...  14.9 us
    unnamed x30, local copies, waits for them, and re-layouts  5.43 us
  transfers between devices with their start and end apart: 31, of which 8 were waited for; matrix products, arithmetic and copies ran while one was open for 5% of the time, Pallas kernels for 15%

profile of v2, /device:TPU:6, one launch (start us, length us, event | category | flops | bytes accessed | tf_op | source)
XLA Modules:
  0.0 212.3 jit_solution(4443490362347633264)
XLA Ops:
  0.6 1.9 collective-permute-start
  2.6 15.1 %collective-permute-start.1 = (bf16[384,768]{1,0:T(8,128)(2,1)}, bf16[384,768]{1,0:T(8,128)(2,1)S(1)}, u32[]{:S(2)}, u32[]{:S(2)}) collective-permute-start(bf16[384,768]{1,0:T(8,128)(2,1)} %bitcast.68), channel_id=1, source_target_pairs={{0,63},{1,0},{2,1},{3,2},{4,3},{5,4},{6,5},{7,6},{8,7},{9,8},{10,9... | collective-permute-start | bytes 1769480 | tf_op jit(solution)/shard_map/ppermute | solution.py:166
  17.6 1.9 collective-permute-start.2
  19.5 12.4 %collective-permute-start.3 = (bf16[384,768]{1,0:T(8,128)(2,1)}, bf16[384,768]{1,0:T(8,128)(2,1)S(1)}, u32[]{:S(2)}, u32[]{:S(2)}) collective-permute-start(bf16[384,768]{1,0:T(8,128)(2,1)} %bitcast.72), channel_id=1, source_target_pairs={{0,63},{1,0},{2,1},{3,2},{4,3},{5,4},{6,5},{7,6},{8,7},{9,8},{10,9... | collective-permute-start | bytes 1769480 | tf_op jit(solution)/shard_map/ppermute | solution.py:166
  33.5 5.0 %collective-permute-start.4 = (bf16[96,384]{1,0:T(8,128)(2,1)}, bf16[96,384]{1,0:T(8,128)(2,1)}, u32[]{:S(2)}, u32[]{:S(2)}) collective-permute-start(bf16[96,384]{1,0:T(8,128)(2,1)} %get-tuple-element.27), channel_id=1, source_target_pairs={{0,64},{64,128},{128,192},{192,0},{256,320},{320,384},{384,448},{4... | collective-permute-start | bytes 221192 | tf_op jit(solution)/shard_map/ppermute | solution.py:166
  40.9 10.4 %collective-permute-start.7 = (bf16[96,384]{1,0:T(8,128)(2,1)}, bf16[96,384]{1,0:T(8,128)(2,1)}, u32[]{:S(2)}, u32[]{:S(2)}) collective-permute-start(bf16[96,384]{1,0:T(8,128)(2,1)} %get-tuple-element.27), channel_id=1, source_target_pairs={{0,256},{64,320},{128,384},{192,448},{256,0},{320,64},{384,128},{4... | collective-permute-start | bytes 221192 | tf_op jit(solution)/shard_map/ppermute | solution.py:166
  52.5 14.9 %fwd.1 = (bf16[6,1152,768]{2,1,0:T(8,128)(2,1)}, f32[6,1,768]{2,1,0:T(1,128)}, bf16[768,384]{1,0:T(8,128)(2,1)}, bf16[2,768,384]{2,1,0:T(8,128)(2,1)}) custom-call(f32[9,768]{1,0:T(8,128)} %reshape.50.bias_ref, bf16[384,768]{1,0:T(8,128)(2,1)} %bitcast.65, bf16[384,768]{1,0:T(8,128)(2,1)} %copy-done.3, bf16[384,768]{1,0:T(8,128)(2,1)} %bitcast.69, ...), custom_call_target="tpu_custom_call" | custom-call | flops 1358954496 | bytes 16777216 | tf_op jit(solution)/shard_map/fwd/pallas_call | solution.py:120
  68.7 1.9 collective-permute-start.16
  70.6 4.3 %collective-permute-start.5 = (bf16[96,384]{1,0:T(8,128)(2,1)}, bf16[96,384]{1,0:T(8,128)(2,1)S(1)}, u32[]{:S(2)}, u32[]{:S(2)}) collective-permute-start(bf16[96,384]{1,0:T(8,128)(2,1)} %get-tuple-element.27), channel_id=1, source_target_pairs={{0,128},{64,192},{128,0},{192,64},{256,384},{320,448},{384,256},{4... | collective-permute-start | bytes 221192 | tf_op jit(solution)/shard_map/ppermute | solution.py:166
  76.9 5.1 %collective-permute-start.8 = (bf16[96,384]{1,0:T(8,128)(2,1)}, bf16[96,384]{1,0:T(8,128)(2,1)S(1)}, u32[]{:S(2)}, u32[]{:S(2)}) collective-permute-start(bf16[96,384]{1,0:T(8,128)(2,1)} %collective-permute-done.7), channel_id=1, source_target_pairs={{0,64},{64,128},{128,192},{192,0},{256,320},{320,384},{384,448},{4... | collective-permute-start | bytes 221192 | tf_op jit(solution)/shard_map/ppermute | solution.py:166
  82.0 1.9 collective-permute-start.9
  84.9 3.3 %collective-permute-start.10 = (bf16[96,384]{1,0:T(8,128)(2,1)}, bf16[96,384]{1,0:T(8,128)(2,1)S(1)}, u32[]{:S(2)}, u32[]{:S(2)}) collective-permute-start(bf16[96,384]{1,0:T(8,128)(2,1)} %collective-permute-done.7), channel_id=1, source_target_pairs={{0,192},{64,0},{128,64},{192,128},{256,448},{320,256},{384,320},{4... | collective-permute-start | bytes 221192 | tf_op jit(solution)/shard_map/ppermute | solution.py:166
  89.5 3.7 %collective-permute-start.17 = (bf16[2,96,384]{2,1,0:T(8,128)(2,1)S(1)}, bf16[2,96,384]{2,1,0:T(8,128)(2,1)S(1)}, u32[]{:S(2)}, u32[]{:S(2)}) collective-permute-start(bf16[2,96,384]{2,1,0:T(8,128)(2,1)S(1)} %get-tuple-element.28), channel_id=1, source_target_pairs={{0,64},{64,128},{128,192},{192,0},{256,320},{320,384},{384,448},{4... | collective-permute-start | bytes 442376 | tf_op jit(solution)/shard_map/ppermute | solution.py:166
  93.2 4.2 %collective-permute-start.18 = (bf16[2,96,384]{2,1,0:T(8,128)(2,1)S(1)}, bf16[2,96,384]{2,1,0:T(8,128)(2,1)S(1)}, u32[]{:S(2)}, u32[]{:S(2)}) collective-permute-start(bf16[2,96,384]{2,1,0:T(8,128)(2,1)S(1)} %get-tuple-element.30), channel_id=1, source_target_pairs={{0,128},{64,192},{128,0},{192,64},{256,384},{320,448},{384,256},{4... | collective-permute-start | bytes 442376 | tf_op jit(solution)/shard_map/ppermute | solution.py:166
  97.4 1.9 collective-permute-start.19
  99.4 1.9 collective-permute-start.11
  102.7 2.9 %collective-permute-done.19 = bf16[2,96,384]{2,1,0:T(8,128)(2,1)S(1)} collective-permute-done((bf16[2,96,384]{2,1,0:T(8,128)(2,1)S(1)}, bf16[2,96,384]{2,1,0:T(8,128)(2,1)S(1)}, u32[]{:S(2)}, u32[]{:S(2)}) %collective-permute-start.19) | collective-permute-done | bytes 147488 | tf_op jit(solution)/shard_map/ppermute | solution.py:166
  105.8 1.9 collective-permute-start.20
  107.7 4.0 %collective-permute-start.21 = (bf16[2,24,384]{2,1,0:T(8,128)(2,1)S(1)}, bf16[2,24,384]{2,1,0:T(8,128)(2,1)S(1)}, u32[]{:S(2)}, u32[]{:S(2)}) collective-permute-start(bf16[2,24,384]{2,1,0:T(8,128)(2,1)S(1)} %get-tuple-element.33), channel_id=1, source_target_pairs={{0,32},{1,33},{2,34},{3,35},{4,36},{5,37},{6,38},{7,39},{8,40},{9,... | collective-permute-start | bytes 110600 | tf_op jit(solution)/shard_map/ppermute | solution.py:166
  111.7 3.3 %collective-permute-start.22 = (bf16[2,24,384]{2,1,0:T(8,128)(2,1)S(1)}, bf16[2,24,384]{2,1,0:T(8,128)(2,1)S(1)}, u32[]{:S(2)}, u32[]{:S(2)}) collective-permute-start(bf16[2,24,384]{2,1,0:T(8,128)(2,1)S(1)} %get-tuple-element.32), channel_id=1, source_target_pairs={{0,48},{1,49},{2,50},{3,51},{4,52},{5,53},{6,54},{7,55},{8,56},{9,... | collective-permute-start | bytes 110600 | tf_op jit(solution)/shard_map/ppermute | solution.py:166
  115.6 2.0 collective-permute-done.22
  117.6 8.7 %collective-permute-start.23 = (bf16[24,384]{1,0:T(8,128)(2,1)S(1)}, bf16[24,384]{1,0:T(8,128)(2,1)S(1)}, u32[]{:S(2)}, u32[]{:S(2)}) collective-permute-start(bf16[24,384]{1,0:T(8,128)(2,1)S(1)} %dynamic-slice_bitcast_fusion.7), channel_id=1, source_target_pairs={{0,256},{64,320},{128,384},{192,448},{256,0},{320,64},{384,128},{4... | collective-permute-start | bytes 55304 | tf_op jit(solution)/shard_map/ppermute | solution.py:166
  127.2 17.5 %bwd.1 = (bf16[384,768]{1,0:T(8,128)(2,1)}, bf16[384,768]{1,0:T(8,128)(2,1)}, f32[384,768]{1,0:T(8,128)}, bf16[384,768]{1,0:T(8,128)(2,1)}, bf16[384,768]{1,0:T(...) custom-call(s32[9]{0:T(128)} %stack.52.place_ref, bf16[384,768]{1,0:T(8,128)(2,1)} %bitcast.66, ...), custom_call_target="tpu_custom_call" | custom-call | flops 2717908992 | bytes 20971520 | tf_op jit(solution)/shard_map/bwd/pallas_call | solution.py:149
  146.6 12.4 %collective-permute-start.15 = (bf16[384,768]{1,0:T(8,128)(2,1)}, bf16[384,768]{1,0:T(8,128)(2,1)S(1)}, u32[]{:S(2)}, u32[]{:S(2)}) collective-permute-start(bf16[384,768]{1,0:T(8,128)(2,1)} %get-tuple-element.24), channel_id=1, source_target_pairs={{0,63},{1,0},{2,1},{3,2},{4,3},{5,4},{6,5},{7,6},{8,7},{9,8},{10,9... | collective-permute-start | bytes 1769480 | tf_op jit(solution)/shard_map/ppermute | solution.py:166
  159.0 1.9 collective-permute-start.24
  160.9 5.8 %collective-permute-done.24 = bf16[24,384]{1,0:T(8,128)(2,1)S(1)} collective-permute-done((bf16[24,384]{1,0:T(8,128)(2,1)S(1)}, bf16[24,384]{1,0:T(8,128)(2,1)S(1)}, u32[]{:S(2)}, u32[]{:S(2)}) %collective-permute-start.24) | collective-permute-done | bytes 18464 | tf_op jit(solution)/shard_map/ppermute | solution.py:166
  170.6 12.4 %collective-permute-start.13 = (bf16[384,768]{1,0:T(8,128)(2,1)}, bf16[384,768]{1,0:T(8,128)(2,1)S(1)}, u32[]{:S(2)}, u32[]{:S(2)}) collective-permute-start(bf16[384,768]{1,0:T(8,128)(2,1)} %get-tuple-element.21), channel_id=1, source_target_pairs={{0,63},{1,0},{2,1},{3,2},{4,3},{5,4},{6,5},{7,6},{8,7},{9,8},{10,9... | collective-permute-start | bytes 1769480 | tf_op jit(solution)/shard_map/ppermute | solution.py:166
  185.0 2.4 %fusion.2 = bf16[1,384,768]{2,1,0:T(8,128)(2,1)} fusion(bf16[384,768]{1,0:T(8,128)(2,1)S(1)} %collective-permute-done.15, f32[384,768]{1,0:T(8,128)} %get-tuple-element.22, bf16[384,768]{1,0:T(8,128)(2,1)S(1)} %collective-permute-done.14), kind=kLoop, calls=%fused_computation.5 | loop fusion | flops 1474560 | bytes 2949120 | tf_op jit(solution)/shard_map/broadcast_in_dim | solution.py:260
  187.3 7.2 %collective-permute-done.26 = bf16[24,384]{1,0:T(8,128)(2,1)S(1)} collective-permute-done((bf16[24,384]{1,0:T(8,128)(2,1)S(1)}, bf16[24,384]{1,0:T(8,128)(2,1)S(1)}, u32[]{:S(2)}, u32[]{:S(2)}) %collective-permute-start.26) | collective-permute-done | bytes 18464 | tf_op jit(solution)/shard_map/ppermute | solution.py:166
  194.6 4.9 %collective-permute-start.27 = (bf16[24,384]{1,0:T(8,128)(2,1)S(1)}, bf16[24,384]{1,0:T(8,128)(2,1)S(1)}, u32[]{:S(2)}, u32[]{:S(2)}) collective-permute-start(bf16[24,384]{1,0:T(8,128)(2,1)S(1)} %add_convert_fusion.2), channel_id=1, source_target_pairs={{0,48},{1,49},{2,50},{3,51},{4,52},{5,53},{6,54},{7,55},{8,56},{9,... | collective-permute-start | bytes 55304 | tf_op jit(solution)/shard_map/ppermute | solution.py:166
  201.5 2.8 %collective-permute-start.29 = (bf16[24,384]{1,0:T(8,128)(2,1)S(1)}, bf16[24,384]{1,0:T(8,128)(2,1)S(1)}, u32[]{:S(2)}, u32[]{:S(2)}) collective-permute-start(bf16[24,384]{1,0:T(8,128)(2,1)S(1)} %add_convert_fusion.2), channel_id=1, source_target_pairs={{0,16},{1,17},{2,18},{3,19},{4,20},{5,21},{6,22},{7,23},{8,24},{9,... | collective-permute-start | bytes 55304 | tf_op jit(solution)/shard_map/ppermute | solution.py:166
  204.3 2.4 %collective-permute-done.28 = bf16[24,384]{1,0:T(8,128)(2,1)S(1)} collective-permute-done((bf16[24,384]{1,0:T(8,128)(2,1)S(1)}, bf16[24,384]{1,0:T(8,128)(2,1)S(1)}, u32[]{:S(2)}, u32[]{:S(2)}) %collective-permute-start.28) | collective-permute-done | bytes 18464 | tf_op jit(solution)/shard_map/ppermute | solution.py:166
  (86 shorter events, 28.6 us)
Async XLA Ops:
  0.6 40.3 %collective-permute-start = (bf16[384,768]{1,0:T(8,128)(2,1)}, bf16[384,768]{1,0:T(8,128)(2,1)S(1)}, u32[]{:S(2)}, u32[]{:S(2)}) collective-permute-start(bf16[384,768]{1,0:T(8,128)(2,1)} %bitcast.67), channel_id=1, source_target_pairs={{0,1},{1,2},{2,3},{3,4},{4,5},{5,6},{6,7},{7,8},{8,9},{9,10},{10,1... | collective-permute-start | bytes 1769480 | tf_op jit(solution)/shard_map/ppermute | solution.py:166
  2.6 48.7 %collective-permute-start.1 = (bf16[384,768]{1,0:T(8,128)(2,1)}, bf16[384,768]{1,0:T(8,128)(2,1)S(1)}, u32[]{:S(2)}, u32[]{:S(2)}) collective-permute-start(bf16[384,768]{1,0:T(8,128)(2,1)} %bitcast.68), channel_id=1, source_target_pairs={{0,63},{1,0},{2,1},{3,2},{4,3},{5,4},{6,5},{7,6},{8,7},{9,8},{10,9... | collective-permute-start | bytes 1769480 | tf_op jit(solution)/shard_map/ppermute | solution.py:166
  17.6 33.7 %collective-permute-start.2 = (bf16[384,768]{1,0:T(8,128)(2,1)}, bf16[384,768]{1,0:T(8,128)(2,1)S(1)}, u32[]{:S(2)}, u32[]{:S(2)}) collective-permute-start(bf16[384,768]{1,0:T(8,128)(2,1)} %bitcast.71), channel_id=1, source_target_pairs={{0,1},{1,2},{2,3},{3,4},{4,5},{5,6},{6,7},{7,8},{8,9},{9,10},{10,1... | collective-permute-start | bytes 1769480 | tf_op jit(solution)/shard_map/ppermute | solution.py:166
  19.5 31.8 %collective-permute-start.3 = (bf16[384,768]{1,0:T(8,128)(2,1)}, bf16[384,768]{1,0:T(8,128)(2,1)S(1)}, u32[]{:S(2)}, u32[]{:S(2)}) collective-permute-start(bf16[384,768]{1,0:T(8,128)(2,1)} %bitcast.72), channel_id=1, source_target_pairs={{0,63},{1,0},{2,1},{3,2},{4,3},{5,4},{6,5},{7,6},{8,7},{9,8},{10,9... | collective-permute-start | bytes 1769480 | tf_op jit(solution)/shard_map/ppermute | solution.py:166
  33.5 48.6 %collective-permute-start.4 = (bf16[96,384]{1,0:T(8,128)(2,1)}, bf16[96,384]{1,0:T(8,128)(2,1)}, u32[]{:S(2)}, u32[]{:S(2)}) collective-permute-start(bf16[96,384]{1,0:T(8,128)(2,1)} %get-tuple-element.27), channel_id=1, source_target_pairs={{0,64},{64,128},{128,192},{192,0},{256,320},{320,384},{384,448},{4... | collective-permute-start | bytes 221192 | tf_op jit(solution)/shard_map/ppermute | solution.py:166
  40.9 36.0 %collective-permute-start.7 = (bf16[96,384]{1,0:T(8,128)(2,1)}, bf16[96,384]{1,0:T(8,128)(2,1)}, u32[]{:S(2)}, u32[]{:S(2)}) collective-permute-start(bf16[96,384]{1,0:T(8,128)(2,1)} %get-tuple-element.27), channel_id=1, source_target_pairs={{0,256},{64,320},{128,384},{192,448},{256,0},{320,64},{384,128},{4... | collective-permute-start | bytes 221192 | tf_op jit(solution)/shard_map/ppermute | solution.py:166
  68.7 20.6 %collective-permute-start.16 = (bf16[768,384]{1,0:T(8,128)(2,1)S(1)}, bf16[768,384]{1,0:T(8,128)(2,1)S(1)}, u32[]{:S(2)}, u32[]{:S(2)}) collective-permute-start(bf16[768,384]{1,0:T(8,128)(2,1)S(1)} %dynamic-slice_bitcast_fusion), channel_id=1, source_target_pairs={{0,1},{1,0},{2,3},{3,2},{4,5},{5,4},{6,7},{7,6},{8,9},{9,8},{10,11... | collective-permute-start | bytes 1769480 | tf_op jit(solution)/shard_map/ppermute | solution.py:166
  70.6 14.3 %collective-permute-start.5 = (bf16[96,384]{1,0:T(8,128)(2,1)}, bf16[96,384]{1,0:T(8,128)(2,1)S(1)}, u32[]{:S(2)}, u32[]{:S(2)}) collective-permute-start(bf16[96,384]{1,0:T(8,128)(2,1)} %get-tuple-element.27), channel_id=1, source_target_pairs={{0,128},{64,192},{128,0},{192,64},{256,384},{320,448},{384,256},{4... | collective-permute-start | bytes 221192 | tf_op jit(solution)/shard_map/ppermute | solution.py:166
  74.9 13.3 %collective-permute-start.6 = (bf16[96,384]{1,0:T(8,128)(2,1)}, bf16[96,384]{1,0:T(8,128)(2,1)S(1)}, u32[]{:S(2)}, u32[]{:S(2)}) collective-permute-start(bf16[96,384]{1,0:T(8,128)(2,1)} %get-tuple-element.27), channel_id=1, source_target_pairs={{0,192},{64,0},{128,64},{192,128},{256,448},{320,256},{384,320},{4... | collective-permute-start | bytes 221192 | tf_op jit(solution)/shard_map/ppermute | solution.py:166
  76.9 12.3 %collective-permute-start.8 = (bf16[96,384]{1,0:T(8,128)(2,1)}, bf16[96,384]{1,0:T(8,128)(2,1)S(1)}, u32[]{:S(2)}, u32[]{:S(2)}) collective-permute-start(bf16[96,384]{1,0:T(8,128)(2,1)} %collective-permute-done.7), channel_id=1, source_target_pairs={{0,64},{64,128},{128,192},{192,0},{256,320},{320,384},{384,448},{4... | collective-permute-start | bytes 221192 | tf_op jit(solution)/shard_map/ppermute | solution.py:166
  82.0 17.3 %collective-permute-start.9 = (bf16[96,384]{1,0:T(8,128)(2,1)}, bf16[96,384]{1,0:T(8,128)(2,1)S(1)}, u32[]{:S(2)}, u32[]{:S(2)}) collective-permute-start(bf16[96,384]{1,0:T(8,128)(2,1)} %collective-permute-done.7), channel_id=1, source_target_pairs={{0,128},{64,192},{128,0},{192,64},{256,384},{320,448},{384,256},{4... | collective-permute-start | bytes 221192 | tf_op jit(solution)/shard_map/ppermute | solution.py:166
  84.9 14.5 %collective-permute-start.10 = (bf16[96,384]{1,0:T(8,128)(2,1)}, bf16[96,384]{1,0:T(8,128)(2,1)S(1)}, u32[]{:S(2)}, u32[]{:S(2)}) collective-permute-start(bf16[96,384]{1,0:T(8,128)(2,1)} %collective-permute-done.7), channel_id=1, source_target_pairs={{0,192},{64,0},{128,64},{192,128},{256,448},{320,256},{384,320},{4... | collective-permute-start | bytes 221192 | tf_op jit(solution)/shard_map/ppermute | solution.py:166
  89.5 11.9 %collective-permute-start.17 = (bf16[2,96,384]{2,1,0:T(8,128)(2,1)S(1)}, bf16[2,96,384]{2,1,0:T(8,128)(2,1)S(1)}, u32[]{:S(2)}, u32[]{:S(2)}) collective-permute-start(bf16[2,96,384]{2,1,0:T(8,128)(2,1)S(1)} %get-tuple-element.28), channel_id=1, source_target_pairs={{0,64},{64,128},{128,192},{192,0},{256,320},{320,384},{384,448},{4... | collective-permute-start | bytes 442376 | tf_op jit(solution)/shard_map/ppermute | solution.py:166
  93.2 9.5 %collective-permute-start.18 = (bf16[2,96,384]{2,1,0:T(8,128)(2,1)S(1)}, bf16[2,96,384]{2,1,0:T(8,128)(2,1)S(1)}, u32[]{:S(2)}, u32[]{:S(2)}) collective-permute-start(bf16[2,96,384]{2,1,0:T(8,128)(2,1)S(1)} %get-tuple-element.30), channel_id=1, source_target_pairs={{0,128},{64,192},{128,0},{192,64},{256,384},{320,448},{384,256},{4... | collective-permute-start | bytes 442376 | tf_op jit(solution)/shard_map/ppermute | solution.py:166
  97.4 8.2 %collective-permute-start.19 = (bf16[2,96,384]{2,1,0:T(8,128)(2,1)S(1)}, bf16[2,96,384]{2,1,0:T(8,128)(2,1)S(1)}, u32[]{:S(2)}, u32[]{:S(2)}) collective-permute-start(bf16[2,96,384]{2,1,0:T(8,128)(2,1)S(1)} %get-tuple-element.29), channel_id=1, source_target_pairs={{0,192},{64,0},{128,64},{192,128},{256,448},{320,256},{384,320},{4... | collective-permute-start | bytes 442376 | tf_op jit(solution)/shard_map/ppermute | solution.py:166
  99.4 26.9 %copy-start.2 = (bf16[768,384]{1,0:T(8,128)(2,1)}, bf16[768,384]{1,0:T(8,128)(2,1)S(1)}, u32[]{:S(2)}) copy-start(bf16[768,384]{1,0:T(8,128)(2,1)S(1)} %constant_dynamic-update-slice_fusion.w_ref) | copy-start | bytes 1769476
  99.4 26.9 %collective-permute-start.11 = (bf16[768,384]{1,0:T(8,128)(2,1)S(1)}, bf16[768,384]{1,0:T(8,128)(2,1)S(1)}, u32[]{:S(2)}, u32[]{:S(2)}) collective-permute-start(bf16[768,384]{1,0:T(8,128)(2,1)S(1)} %constant_dynamic-update-slice_fusion.w_ref), channel_id=1, source_target_pairs={{0,1},{1,0},{2,3},{3,2},{4,5},{5,4},{6,7},{7,6},{8,9},{9,8},{10,11... | collective-permute-start | bytes 1769480 | tf_op jit(solution)/shard_map/ppermute | solution.py:166
  105.8 9.8 %collective-permute-start.20 = (bf16[2,24,384]{2,1,0:T(8,128)(2,1)S(1)}, bf16[2,24,384]{2,1,0:T(8,128)(2,1)S(1)}, u32[]{:S(2)}, u32[]{:S(2)}) collective-permute-start(bf16[2,24,384]{2,1,0:T(8,128)(2,1)S(1)} %get-tuple-element.31), channel_id=1, source_target_pairs={{0,16},{1,17},{2,18},{3,19},{4,20},{5,21},{6,22},{7,23},{8,24},{9,... | collective-permute-start | bytes 110600 | tf_op jit(solution)/shard_map/ppermute | solution.py:166
  107.7 7.9 %collective-permute-start.21 = (bf16[2,24,384]{2,1,0:T(8,128)(2,1)S(1)}, bf16[2,24,384]{2,1,0:T(8,128)(2,1)S(1)}, u32[]{:S(2)}, u32[]{:S(2)}) collective-permute-start(bf16[2,24,384]{2,1,0:T(8,128)(2,1)S(1)} %get-tuple-element.33), channel_id=1, source_target_pairs={{0,32},{1,33},{2,34},{3,35},{4,36},{5,37},{6,38},{7,39},{8,40},{9,... | collective-permute-start | bytes 110600 | tf_op jit(solution)/shard_map/ppermute | solution.py:166
  111.7 5.9 %collective-permute-start.22 = (bf16[2,24,384]{2,1,0:T(8,128)(2,1)S(1)}, bf16[2,24,384]{2,1,0:T(8,128)(2,1)S(1)}, u32[]{:S(2)}, u32[]{:S(2)}) collective-permute-start(bf16[2,24,384]{2,1,0:T(8,128)(2,1)S(1)} %get-tuple-element.32), channel_id=1, source_target_pairs={{0,48},{1,49},{2,50},{3,51},{4,52},{5,53},{6,54},{7,55},{8,56},{9,... | collective-permute-start | bytes 110600 | tf_op jit(solution)/shard_map/ppermute | solution.py:166
  117.6 41.4 %collective-permute-start.23 = (bf16[24,384]{1,0:T(8,128)(2,1)S(1)}, bf16[24,384]{1,0:T(8,128)(2,1)S(1)}, u32[]{:S(2)}, u32[]{:S(2)}) collective-permute-start(bf16[24,384]{1,0:T(8,128)(2,1)S(1)} %dynamic-slice_bitcast_fusion.7), channel_id=1, source_target_pairs={{0,256},{64,320},{128,384},{192,448},{256,0},{320,64},{384,128},{4... | collective-permute-start | bytes 55304 | tf_op jit(solution)/shard_map/ppermute | solution.py:166
  144.7 40.3 %collective-permute-start.14 = (bf16[384,768]{1,0:T(8,128)(2,1)}, bf16[384,768]{1,0:T(8,128)(2,1)S(1)}, u32[]{:S(2)}, u32[]{:S(2)}) collective-permute-start(bf16[384,768]{1,0:T(8,128)(2,1)} %get-tuple-element.23), channel_id=1, source_target_pairs={{0,1},{1,2},{2,3},{3,4},{4,5},{5,6},{6,7},{7,8},{8,9},{9,10},{10,1... | collective-permute-start | bytes 1769480 | tf_op jit(solution)/shard_map/ppermute | solution.py:166
  146.6 38.4 %collective-permute-start.15 = (bf16[384,768]{1,0:T(8,128)(2,1)}, bf16[384,768]{1,0:T(8,128)(2,1)S(1)}, u32[]{:S(2)}, u32[]{:S(2)}) collective-permute-start(bf16[384,768]{1,0:T(8,128)(2,1)} %get-tuple-element.24), channel_id=1, source_target_pairs={{0,63},{1,0},{2,1},{3,2},{4,3},{5,4},{6,5},{7,6},{8,7},{9,8},{10,9... | collective-permute-start | bytes 1769480 | tf_op jit(solution)/shard_map/ppermute | solution.py:166
  159.0 7.8 %collective-permute-start.24 = (bf16[24,384]{1,0:T(8,128)(2,1)S(1)}, bf16[24,384]{1,0:T(8,128)(2,1)S(1)}, u32[]{:S(2)}, u32[]{:S(2)}) collective-permute-start(bf16[24,384]{1,0:T(8,128)(2,1)S(1)} %fusion.10), channel_id=1, source_target_pairs={{0,2},{1,3},{2,0},{3,1},{4,6},{5,7},{6,4},{7,5},{8,10},{9,11},{10,... | collective-permute-start | bytes 55304 | tf_op jit(solution)/shard_map/ppermute | solution.py:166
  166.8 16.2 %collective-permute-start.25 = (bf16[24,384]{1,0:T(8,128)(2,1)S(1)}, bf16[24,384]{1,0:T(8,128)(2,1)S(1)}, u32[]{:S(2)}, u32[]{:S(2)}) collective-permute-start(bf16[24,384]{1,0:T(8,128)(2,1)S(1)} %add_convert_fusion.4), channel_id=1, source_target_pairs={{0,4},{1,5},{2,6},{3,7},{4,0},{5,1},{6,2},{7,3},{8,12},{9,13},{10,... | collective-permute-start | bytes 55304 | tf_op jit(solution)/shard_map/ppermute | solution.py:166
  168.7 41.6 %collective-permute-start.12 = (bf16[384,768]{1,0:T(8,128)(2,1)}, bf16[384,768]{1,0:T(8,128)(2,1)S(1)}, u32[]{:S(2)}, u32[]{:S(2)}) collective-permute-start(bf16[384,768]{1,0:T(8,128)(2,1)} %get-tuple-element.20), channel_id=1, source_target_pairs={{0,1},{1,2},{2,3},{3,4},{4,5},{5,6},{6,7},{7,8},{8,9},{9,10},{10,1... | collective-permute-start | bytes 1769480 | tf_op jit(solution)/shard_map/ppermute | solution.py:166
  170.6 39.7 %collective-permute-start.13 = (bf16[384,768]{1,0:T(8,128)(2,1)}, bf16[384,768]{1,0:T(8,128)(2,1)S(1)}, u32[]{:S(2)}, u32[]{:S(2)}) collective-permute-start(bf16[384,768]{1,0:T(8,128)(2,1)} %get-tuple-element.21), channel_id=1, source_target_pairs={{0,63},{1,0},{2,1},{3,2},{4,3},{5,4},{6,5},{7,6},{8,7},{9,8},{10,9... | collective-permute-start | bytes 1769480 | tf_op jit(solution)/shard_map/ppermute | solution.py:166
  183.0 11.6 %collective-permute-start.26 = (bf16[24,384]{1,0:T(8,128)(2,1)S(1)}, bf16[24,384]{1,0:T(8,128)(2,1)S(1)}, u32[]{:S(2)}, u32[]{:S(2)}) collective-permute-start(bf16[24,384]{1,0:T(8,128)(2,1)S(1)} %add_convert_fusion.3), channel_id=1, source_target_pairs={{0,8},{1,9},{2,10},{3,11},{4,12},{5,13},{6,14},{7,15},{8,0},{9,1},... | collective-permute-start | bytes 55304 | tf_op jit(solution)/shard_map/ppermute | solution.py:166
  194.6 9.6 %collective-permute-start.27 = (bf16[24,384]{1,0:T(8,128)(2,1)S(1)}, bf16[24,384]{1,0:T(8,128)(2,1)S(1)}, u32[]{:S(2)}, u32[]{:S(2)}) collective-permute-start(bf16[24,384]{1,0:T(8,128)(2,1)S(1)} %add_convert_fusion.2), channel_id=1, source_target_pairs={{0,48},{1,49},{2,50},{3,51},{4,52},{5,53},{6,54},{7,55},{8,56},{9,... | collective-permute-start | bytes 55304 | tf_op jit(solution)/shard_map/ppermute | solution.py:166
  199.5 7.2 %collective-permute-start.28 = (bf16[24,384]{1,0:T(8,128)(2,1)S(1)}, bf16[24,384]{1,0:T(8,128)(2,1)S(1)}, u32[]{:S(2)}, u32[]{:S(2)}) collective-permute-start(bf16[24,384]{1,0:T(8,128)(2,1)S(1)} %add_convert_fusion.2), channel_id=1, source_target_pairs={{0,32},{1,33},{2,34},{3,35},{4,36},{5,37},{6,38},{7,39},{8,40},{9,... | collective-permute-start | bytes 55304 | tf_op jit(solution)/shard_map/ppermute | solution.py:166
  201.5 6.9 %collective-permute-start.29 = (bf16[24,384]{1,0:T(8,128)(2,1)S(1)}, bf16[24,384]{1,0:T(8,128)(2,1)S(1)}, u32[]{:S(2)}, u32[]{:S(2)}) collective-permute-start(bf16[24,384]{1,0:T(8,128)(2,1)S(1)} %add_convert_fusion.2), channel_id=1, source_target_pairs={{0,16},{1,17},{2,18},{3,19},{4,20},{5,21},{6,22},{7,23},{8,24},{9,... | collective-permute-start | bytes 55304 | tf_op jit(solution)/shard_map/ppermute | solution.py:166
  208.4 3.2 %collective-permute-start.30 = (bf16[96,384]{1,0:T(8,128)(2,1)S(1)}, bf16[96,384]{1,0:T(8,128)(2,1)S(1)}, u32[]{:S(2)}, u32[]{:S(2)}) collective-permute-start(bf16[96,384]{1,0:T(8,128)(2,1)S(1)} %bitcast.79), channel_id=1, source_target_pairs={{0,1},{1,0},{2,3},{3,2},{4,5},{5,4},{6,7},{7,6},{8,9},{9,8},{10,11... | collective-permute-start | bytes 221192 | tf_op jit(solution)/shard_map/ppermute | solution.py:166
  (7 other events, 61.4 us)
